TPU v7x, 128 devices: a whole 4x4x4 slice. The times are simulated.
128 devices in a mesh: ping: 16 (over x, z), band: 8 (over y, core).
Axes of the slice: x: 4, y: 4, z: 4, core: 2. Of those that a mesh axis runs over, the one named last changes fastest.
Arguments:
- echoes: bfloat16 [2048, 8, 2, 8192], P(('ping', 'band')), may hold values from -6 to 6
- replica: bfloat16 [8, 2, 128], replicated, may hold values from -0.375 to 0.375
- steering: bfloat16 [2, 64, 64], replicated, may hold values from -0.5 to 0.5
- angle_weights: bfloat16 [2, 128, 64], replicated, may hold values from -0.75 to 0.75
- range_weights: bfloat16 [64, 384, 128], P('band'), may hold values from -0.3125 to 0.3125
- range_offsets: int32 [64], P('band'), may hold values from 0 to 5
- merge_owner: int32 [256], replicated, may hold values from -1 to 15, as said below
- merge_slot: int32 [256], replicated, may hold values from 0 to 7
Outputs:
- merged: bfloat16 [128, 2, 128, 8192], P('ping', None, None, 'band')
Inputs may be any that keep to these rules, and one draw needn't show every extreme that they name: `merge_owner`: -1 marks a block that is not kept. Among the 16 blocks of one ping index (aligned blocks of the list) at most 2 name the same owner, and in every draw one owner is named by exactly 2 blocks of every ping index.
All inputs are finite; a program needn't handle non-finite values.
Results may differ from a plain program's by a relative error of at most 0.007.
Values may be sent and summed in bfloat16 or wider, within the bound.
No kernel may reach another device: no remote copies, remote signals or barrier semaphores. Data moves between devices by JAX's collectives and lax.ppermute only.
A program may use at most 128 MiB of HBM per device.

v0:
```python
import jax
import jax.numpy as jnp
from jax import lax
from jax.sharding import PartitionSpec as P

SUB_PINGS = 8


def toeplitz_blocks(replica):
    taps_count = replica.shape[2]
    shifts = jnp.arange(taps_count)
    row_index = jnp.arange(taps_count)[:, None]
    col_index = jnp.arange(taps_count)[None, :]
    lower_sel = ((row_index - col_index)[None] == shifts[:, None, None]).astype(jnp.float32)
    upper_sel = ((row_index - col_index + taps_count)[None] == shifts[:, None, None]).astype(
        jnp.float32
    )
    real_taps = replica[:, 0].astype(jnp.float32)
    imag_taps = replica[:, 1].astype(jnp.float32)
    high = lax.Precision.HIGHEST
    lower_real = jnp.einsum("ck,kmn->cmn", real_taps, lower_sel, precision=high)
    lower_imag = jnp.einsum("ck,kmn->cmn", imag_taps, lower_sel, precision=high)
    upper_real = jnp.einsum("ck,kmn->cmn", real_taps, upper_sel, precision=high)
    upper_imag = jnp.einsum("ck,kmn->cmn", imag_taps, upper_sel, precision=high)
    layers = [
        jnp.concatenate([lower_real, -lower_imag], 2),
        jnp.concatenate([lower_imag, lower_real], 2),
        jnp.concatenate([upper_real, -upper_imag], 2),
        jnp.concatenate([upper_imag, upper_real], 2),
    ]
    return jnp.concatenate(layers, 1).astype(jnp.bfloat16)


def compress(echo_part, toeplitz):
    pings, chans, parts, bins = echo_part.shape
    taps_count = toeplitz.shape[2] // 2
    block_count = bins // taps_count
    shaped = echo_part.reshape(pings, chans, parts, block_count, taps_count)
    weights = toeplitz.reshape(chans, 2, parts, taps_count, 2, taps_count)
    lower = jnp.einsum(
        "pcqbk,cqkon->pcobn", shaped, weights[:, 0], preferred_element_type=jnp.float32
    )
    upper = jnp.einsum(
        "pcqbk,cqkon->pcobn", shaped, weights[:, 1], preferred_element_type=jnp.float32
    )
    moved = jnp.concatenate([upper[:, :, :, 1:], jnp.zeros_like(upper[:, :, :, :1])], axis=3)
    total = lower + moved
    return total.reshape(pings, chans, 2, bins).astype(jnp.bfloat16)


def beamform(tile, steering, sub_pings):
    pings, chans, parts, bins = tile.shape
    blocks = pings // sub_pings
    grouped = tile.reshape(blocks, sub_pings * chans * parts, bins)
    real_steer = steering[0]
    imag_steer = steering[1]
    beam_count = real_steer.shape[0]
    mixer = jnp.concatenate(
        [
            jnp.concatenate([real_steer, -imag_steer], 1),
            jnp.concatenate([imag_steer, real_steer], 1),
        ],
        0,
    )
    mixer = (
        mixer.reshape(2 * beam_count, 2, sub_pings * chans)
        .transpose(0, 2, 1)
        .reshape(2 * beam_count, -1)
    )
    beams = jnp.einsum("yx,bxr->byr", mixer, grouped, preferred_element_type=jnp.float32)
    return beams.reshape(blocks, 2, beam_count, bins).astype(jnp.bfloat16)


def rotate_angles(beam_image, angle_weights, parity):
    matrices = jnp.where(parity[:, None, None] == 1, angle_weights[1], angle_weights[0])
    turned = jnp.einsum("bya,bpar->bpyr", matrices, beam_image, preferred_element_type=jnp.float32)
    return turned.astype(jnp.bfloat16)


def dense_interp(range_weights, range_offsets):
    count = range_weights.shape[0]
    selector = (
        jnp.arange(count)[None, None, :]
        == (range_offsets[:, None] + jnp.arange(3)[None, :])[:, :, None]
    ).astype(jnp.bfloat16)
    pieces = range_weights.reshape(count, 3, 128, 128)
    dense = jnp.einsum("jtb,jtin->bijn", selector, pieces, preferred_element_type=jnp.float32)
    return dense.astype(jnp.bfloat16).reshape(count * 128, count * 128)


def range_interp(turned, dense):
    flat = turned.reshape(-1, turned.shape[3])
    product = jnp.dot(flat, dense, preferred_element_type=jnp.float32)
    return product.astype(jnp.bfloat16).reshape(turned.shape)


def pack_rows(packer, source):
    flat = jnp.dot(packer, source.reshape(source.shape[0], -1), preferred_element_type=jnp.float32)
    return flat.astype(jnp.bfloat16).reshape((packer.shape[0],) + source.shape[1:])


def on_device(
    echoes, replica, steering, angle_weights, range_weights, range_offsets, merge_owner, merge_slot
):
    ping_count = lax.axis_size("ping")
    ping_index = lax.axis_index("ping")
    toeplitz = toeplitz_blocks(replica)
    compressed = compress(echoes, toeplitz)
    band_tile = lax.all_to_all(compressed, "band", split_axis=3, concat_axis=0, tiled=True)
    beam_image = beamform(band_tile, steering, SUB_PINGS)
    blocks_here = beam_image.shape[0]
    capacity = max(2, (blocks_here + ping_count - 1) // ping_count)
    slot_count = blocks_here // 2
    routes = merge_owner.reshape(ping_count, blocks_here)
    slots_all = merge_slot.reshape(ping_count, blocks_here)
    my_routes = lax.dynamic_index_in_dim(routes, ping_index, 0, keepdims=False)
    target_hot = (my_routes[:, None] == jnp.arange(ping_count)[None, :]).astype(jnp.int32)
    rank_send = jnp.sum(jnp.cumsum(target_hot, 0) * target_hot, 1) - 1
    packer = (target_hot.T[:, None, :] == 1) & (
        rank_send[None, None, :] == jnp.arange(capacity)[None, :, None]
    )
    packer = packer.reshape(ping_count * capacity, blocks_here).astype(jnp.bfloat16)
    owned = (routes == ping_index).astype(jnp.int32)
    rank_recv = jnp.cumsum(owned, 1) * owned - 1
    matched = (owned[:, None, :] == 1) & (
        rank_recv[:, None, :] == jnp.arange(capacity)[None, :, None]
    )
    matched_float = matched.astype(jnp.float32)
    slot_hot = (slots_all[:, :, None] == jnp.arange(slot_count)[None, None, :]).astype(jnp.float32)
    combiner = jnp.einsum("scb,sbo->osc", matched_float, slot_hot).reshape(
        slot_count, ping_count * capacity
    )
    combiner = combiner.astype(jnp.bfloat16)
    dense = dense_interp(range_weights, range_offsets)
    my_parity = (ping_index * blocks_here + jnp.arange(blocks_here)) % 2
    images = range_interp(rotate_angles(beam_image, angle_weights, my_parity), dense)
    outgoing = pack_rows(packer, images)
    arrived = lax.all_to_all(outgoing, "ping", split_axis=0, concat_axis=0, tiled=True)
    merged = jnp.dot(
        combiner, arrived.reshape(arrived.shape[0], -1), preferred_element_type=jnp.float32
    )
    return merged.reshape((slot_count,) + arrived.shape[1:]).astype(jnp.bfloat16)


def solution(mesh):
    placed = (
        P(("ping", "band"), None, None, None),
        P(),
        P(),
        P(),
        P("band", None, None),
        P("band"),
        P(),
        P(),
    )
    return jax.shard_map(
        on_device,
        mesh=mesh,
        in_specs=placed,
        out_specs=P("ping", None, None, "band"),
        check_vma=False,
    )
```

profile of v0, /device:TPU:68, one launch (start us, length us, event | category | flops | bytes accessed | tf_op | source)
XLA Modules:
  0.0 673.8 jit_solution(3247890180094275025)
XLA Ops:
  0.0 0.8 fusion.50
  0.8 1.3 fusion.3
  2.2 1.3 fusion.27
  3.5 1.3 fusion.28
  4.8 1.4 fusion.30
  6.3 9.8 %maximum_maximum_fusion = bf16[8,512,256]{2,0,1:T(8,128)(2,1)S(1)} fusion(bf16[8,128,128]{2,0,1:T(8,128)(2,1)S(1)} %fusion.27, bf16[8,128,128]{2,0,1:T(8,128)(2,1)S(1)} %get-tuple-element.21, bf16[8,128,128]{2,0,1:T(8,128)(2,1)S(1)} %get-tuple-element.22, bf16[8,128,128]{2,0,1:T(8,128)(2,1)S(1)} %fusion.28, bf16[8,128,128]{2,0,1:T(8,128)(2,1)S(1)} %get-tuple-element.10, ...), kind=kLoop, calls=%fused_computation.26 | loop fusion | flops 16777216 | bytes 3670016 | tf_op jit(solution)/shard_map/concatenate | solution.py:31
  16.1 0.4 fusion.48
  16.5 7.8 %reshape.188 = bf16[16,8,2,64,128]{4,3,2,1,0:T(8,128)(2,1)} reshape(bf16[16,8,2,8192]{3,2,1,0:T(2,128)(2,1)} %param.8) | data formatting | bytes 8388608 | tf_op jit(solution)/shard_map/reshape | solution.py:38
  24.3 6.7 fusion.15
  31.0 4.7 slice.38
  35.6 2.9 fusion.2
  38.6 48.6 %copy.68 = bf16[16,8,2,64,128]{0,2,1,4,3:T(2,128)(2,1)} copy(bf16[16,8,2,64,128]{4,3,0,2,1:T(8,128)(2,1)} %fusion.2) | data formatting | bytes 8388608 | tf_op jit(solution)/shard_map/convert_element_type | solution.py:48
  87.2 37.8 %reshape.209 = bf16[8,2,131072]{2,1,0:T(2,128)(2,1)} reshape(bf16[8192,8,2,16]{3,2,1,0:T(2,128)(2,1)} %bitcast.128) | data formatting | bytes 8388608
  125.1 4.7 all-to-all-start
  130.3 1.2 convert_bitcast_fusion
  131.5 2.7 copy.49
  134.4 0.2 select_reduce_fusion
  134.7 44.8 %all-to-all-done = bf16[8,2,131072]{2,1,0:T(2,128)(2,1)} async-done(((bf16[8,2,131072]{2,1,0:T(2,128)(2,1)}), bf16[8,2,131072]{2,1,0:T(2,128)(2,1)}, u32[]{:S(2)}, u32[]{:S(2)}) %all-to-all-start) | async-done | bytes 4194336 | tf_op jit(solution)/shard_map/all_to_all | solution.py:109
  179.4 25.7 %reshape.210 = bf16[8192,8,2,16]{3,2,1,0:T(2,128)(2,1)} reshape(bf16[8,2,131072]{2,1,0:T(2,128)(2,1)} %all-to-all-done) | data formatting | bytes 8388608
  205.2 76.8 %copy.43 = bf16[16,8,2,8,1024]{4,2,1,0,3:T(2,128)(2,1)} copy(bf16[16,8,2,8,1024]{0,2,1,4,3:T(2,128)(2,1)} %bitcast.129) | data formatting | bytes 8388608 | tf_op jit(solution)/shard_map/all_to_all | solution.py:109
  282.0 7.2 %reshape.189 = bf16[16,128,1024]{2,1,0:T(8,128)(2,1)} reshape(bf16[8,16,8,2,1024]{4,3,2,1,0:T(2,128)(2,1)} %bitcast.132) | data formatting | bytes 8388608 | tf_op jit(solution)/shard_map/reshape | solution.py:54
  289.2 3.7 convolution_convert_fusion.3
  292.9 2.4 convolution_convert_fusion.2
  295.4 12.4 %convolution_convert_fusion.1 = bf16[4096,1024]{1,0:T(8,128)(2,1)} fusion(bf16[4096,1024]{1,0:T(8,128)(2,1)S(1)} %bitcast.134, bf16[128,8,8,128]{3,2,1,0:T(8,128)(2,1)} %bitcast.136), kind=kOutput, calls=%fused_computation.11 | convolution fusion | flops 8594128896 | bytes 18874368 | tf_op jit(solution)/shard_map/dot_general | solution.py:93
  307.8 8.1 %reshape_reshape.3 = bf16[16,262144]{1,0:T(8,128)(2,1)} reshape(bf16[4096,1024]{1,0:T(8,128)(2,1)} %convolution_convert_fusion.1) | data formatting | bytes 16777216 | tf_op jit(solution)/shard_map/reshape;reshape | solution.py:98
  316.0 13.6 %convolution_convert_fusion = bf16[32,262144]{1,0:T(8,128)(2,1)} fusion(pred[32,16]{1,0:T(32,128)(4,1)S(1)} %and.49, bf16[16,262144]{1,0:T(8,128)(2,1)} %reshape_reshape.3), kind=kOutput, calls=%fused_computation | convolution fusion | flops 276824064 | bytes 25166336 | tf_op jit(solution)/shard_map/dot_general | solution.py:98
  329.5 18.7 %copy.77 = bf16[4,8,256,1024]{3,2,1,0:T(8,128)(2,1)} copy(bf16[4,8,256,1024]{3,1,2,0:T(8,128)(2,1)} %bitcast.131) | data formatting | bytes 33554432
  348.3 7.9 %all-to-all-start.1 = ((bf16[32,2,128,1024]{3,2,1,0:T(8,128)(2,1)}), bf16[32,2,128,1024]{3,2,1,0:T(8,128)(2,1)}, u32[]{:S(2)}, u32[]{:S(2)}) async-start(bf16[32,2,128,1024]{3,2,1,0:T(8,128)(2,1)} %bitcast.130), calls=%async_computation.1 | async-start | bytes 33554432 | tf_op jit(solution)/shard_map/all_to_all | solution.py:138
  356.2 0.2 reduce_window_sum.22
  356.6 295.7 %all-to-all-done.1 = bf16[32,2,128,1024]{3,2,1,0:T(8,128)(2,1)} async-done(((bf16[32,2,128,1024]{3,2,1,0:T(8,128)(2,1)}), bf16[32,2,128,1024]{3,2,1,0:T(8,128)(2,1)}, u32[]{:S(2)}, u32[]{:S(2)}) %all-to-all-start.1) | async-done | bytes 16777248 | tf_op jit(solution)/shard_map/all_to_all | solution.py:138
  652.3 16.6 %fusion.20 = bf16[8,2,128,1024]{3,0,2,1:T(8,128)(2,1)S(1)} fusion(bf16[8,32,1,1]{0,1,3,2:T(8,128)(2,1)S(1)} %bitcast.141, bf16[2,128,1024,32]{2,1,0,3:T(8,128)(2,1)} %bitcast.76), kind=kOutput, calls=%fused_computation.22 | convolution fusion | flops 136314880 | bytes 20972032 | tf_op jit(solution)/shard_map/dot_general | solution.py:139
  669.0 4.4 copy.52
  (40 shorter events, 1.0 us)
Async XLA Ops:
  0.0 130.3 %copy-start = (bf16[8,384,128]{2,1,0:T(8,128)(2,1)S(1)}, bf16[8,384,128]{2,1,0:T(8,128)(2,1)}, u32[]{:S(2)}) copy-start(bf16[8,384,128]{2,1,0:T(8,128)(2,1)} %param.12) | copy-start | bytes 2359300
  31.0 4.7 copy-start.2
  125.1 4.7 copy-start.3
  125.1 5.1 copy-start.7
  125.1 54.4 %all-to-all-start = ((bf16[8,2,131072]{2,1,0:T(2,128)(2,1)}), bf16[8,2,131072]{2,1,0:T(2,128)(2,1)}, u32[]{:S(2)}, u32[]{:S(2)}) async-start(bf16[8,2,131072]{2,1,0:T(2,128)(2,1)} %reshape.209), calls=%async_computation | async-start | bytes 8388608 | tf_op jit(solution)/shard_map/all_to_all | solution.py:109
  129.8 4.4 copy-start.5
  129.8 4.8 copy-start.4
  348.3 8.1 %copy-start.6 = (s32[256]{0:T(256)S(1)}, s32[256]{0:T(256)}, u32[]{:S(2)}) copy-start(s32[256]{0:T(256)} %param.15) | copy-start | bytes 3076
  348.3 304.1 %all-to-all-start.1 = ((bf16[32,2,128,1024]{3,2,1,0:T(8,128)(2,1)}), bf16[32,2,128,1024]{3,2,1,0:T(8,128)(2,1)}, u32[]{:S(2)}, u32[]{:S(2)}) async-start(bf16[32,2,128,1024]{3,2,1,0:T(8,128)(2,1)} %bitcast.130), calls=%async_computation.1 | async-start | bytes 33554432 | tf_op jit(solution)/shard_map/all_to_all | solution.py:138
  652.3 21.0 %copy-start.1 = (bf16[8,384,128]{2,1,0:T(8,128)(2,1)S(1)}, bf16[8,384,128]{2,1,0:T(8,128)(2,1)}, u32[]{:S(2)}) copy-start(bf16[8,384,128]{2,1,0:T(8,128)(2,1)} %param.12) | copy-start | bytes 2359300
where the time goes:
time: 684 us; the launch traced here: 674 us
  waiting for transfers between devices  340 us (50%)
  local copies, waits for them, and re-layouts  244 us (36%)
  matrix products  65.2 us (10%)
  starting transfers between devices  12.6 us (2%)
  other arithmetic  10.5 us (2%)
    all_to_all x1, waiting for transfers between devices, on_device(): lax.all_to_all(outgoing, 'ping', split_axis=0, concat_axis=0, tiled=True)  296 us
    unnamed x21, local copies, waits for them, and re-layouts  82.5 us
    all_to_all x1, local copies, waits for them, and re-layouts, on_device(): lax.all_to_all(compressed, 'band', split_axis=3, concat_axis=0, tiled=True)  76.8 us
    convert_element_type x1, local copies, waits for them, and re-layouts, compress(): return total.reshape(pings, chans, 2, bins).astype(jnp.bfloat16)  48.6 us
    all_to_all x1, waiting for transfers between devices, on_device(): lax.all_to_all(compressed, 'band', split_axis=3, concat_axis=0, tiled=True)  44.8 us
    dot_general x1, matrix products, on_device(): jnp.dot(combiner, arrived.reshape(arrived.shape[0], -1), preferred_elemen...  16.6 us
  transfers between devices with their start and end apart: 2, of which 2 were waited for; matrix products, arithmetic and copies ran while one was open for 1% of the time, Pallas kernels for 0%

commit v1 on v0

--- a/solution.py
+++ b/solution.py
@@ -106,7 +106,12 @@
     ping_index = lax.axis_index("ping")
     toeplitz = toeplitz_blocks(replica)
     compressed = compress(echoes, toeplitz)
-    band_tile = lax.all_to_all(compressed, "band", split_axis=3, concat_axis=0, tiled=True)
+    band_tile = jnp.concatenate(
+        lax.all_to_all(
+            jnp.stack(jnp.split(compressed, lax.axis_size("band"), axis=3)), "band", 0, 0
+        ),
+        axis=0,
+    )
     beam_image = beamform(band_tile, steering, SUB_PINGS)
     blocks_here = beam_image.shape[0]
     capacity = max(2, (blocks_here + ping_count - 1) // ping_count)

time: 684 us -> 522 us (0.76)
  local copies, waits for them, and re-layouts: 244 us -> 85.9 us
    all_to_all x1, local copies, waits for them, and re-layouts: 76.8 us -> 8.57 us  [on_device(): lax.all_to_all(jnp.stack(jnp.split(compressed, lax.axis_size('band'), axi...]
    unnamed x21 -> x26, local copies, waits for them, and re-layouts: 82.5 us -> 32.1 us
    convert_element_type x1, local copies, waits for them, and re-layouts: 48.6 us -> 7.31 us  [compress(): return total.reshape(pings, chans, 2, bins).astype(jnp.bfloat16)]
    another operation x0 -> x2, local copies, waits for them, and re-layouts: none -> 9.1 us  [the longest x1 7.22 us: beamform(): grouped = tile.reshape(blocks, sub_pings * chans * parts, bins)]
    reshape x1 -> x0, local copies, waits for them, and re-layouts: 7.22 us -> none  [beamform(): grouped = tile.reshape(blocks, sub_pings * chans * parts, bins)]
where the time goes in v1:
time: 522 us; the launch traced here: 516 us
  waiting for transfers between devices  341 us (65%)
  local copies, waits for them, and re-layouts  85.9 us (16%)
  matrix products  65.4 us (13%)
  starting transfers between devices  12.8 us (2%)
  other arithmetic  10.5 us (2%)
    all_to_all x1, waiting for transfers between devices, on_device(): lax.all_to_all(outgoing, 'ping', split_axis=0, concat_axis=0, tiled=True)  296 us
    all_to_all x1, waiting for transfers between devices, on_device(): lax.all_to_all(jnp.stack(jnp.split(compressed, lax.axis_size('band'), axi...  44.8 us
    unnamed x26, local copies, waits for them, and re-layouts  32.1 us
    dot_general x1, matrix products, on_device(): jnp.dot(combiner, arrived.reshape(arrived.shape[0], -1), preferred_elemen...  16.6 us
    dot_general x1, matrix products, pack_rows(): jnp.dot(packer, source.reshape(source.shape[0], -1), preferred_element_ty...  13.6 us
    dot_general x1, matrix products, range_interp(): product = jnp.dot(flat, dense, preferred_element_type=jnp.float32)  12.6 us
  transfers between devices with their start and end apart: 2, of which 2 were waited for; matrix products, arithmetic and copies ran while one was open for 1% of the time, Pallas kernels for 0%

profile of v1, /device:TPU:68, one launch (start us, length us, event | category | flops | bytes accessed | tf_op | source)
XLA Modules:
  0.0 516.0 jit_solution(7477339273675361191)
XLA Ops:
  0.8 1.3 fusion.28
  2.2 1.3 fusion.27
  4.8 1.4 fusion.38
  6.3 9.8 %maximum_maximum_fusion = bf16[8,512,256]{2,0,1:T(8,128)(2,1)S(1)} fusion(bf16[8,128,128]{2,0,1:T(8,128)(2,1)S(1)} %fusion.27, bf16[8,128,128]{2,0,1:T(8,128)(2,1)S(1)} %get-tuple-element.21, bf16[8,128,128]{2,0,1:T(8,128)(2,1)S(1)} %get-tuple-element.22, bf16[8,128,128]{2,0,1:T(8,128)(2,1)S(1)} %fusion.28, bf16[8,128,128]{2,0,1:T(8,128)(2,1)S(1)} %get-tuple-element.10, ...), kind=kLoop, calls=%fused_computation.26 | loop fusion | flops 16777216 | bytes 3670016 | tf_op jit(solution)/shard_map/concatenate | solution.py:31
  16.5 7.8 %reshape.184 = bf16[16,8,2,64,128]{4,3,2,1,0:T(8,128)(2,1)} reshape(bf16[16,8,2,8192]{3,2,1,0:T(2,128)(2,1)} %param.8) | data formatting | bytes 8388608 | tf_op jit(solution)/shard_map/reshape | solution.py:38
  24.3 6.7 %fusion.15 = f32[16,8,2,64,128]{4,3,0,2,1:T(8,128)} fusion(bf16[8,1,2,128,2,128]{5,0,4,3,2,1:T(8,128)(2,1)S(1)} %get-tuple-element.8, bf16[16,8,2,64,128]{4,3,2,1,0:T(8,128)(2,1)} %reshape.184), kind=kOutput, calls=%fused_computation.21 | convolution fusion | flops 1073741824 | bytes 13631488 | tf_op jit(solution)/shard_map/pcqbk,cqkon->pcobn/dot_general | solution.py:43
  31.0 4.7 slice.38
  35.6 2.9 fusion.2
  38.6 7.3 %convert_element_type.87 = bf16[16,8,2,8192]{3,0,2,1:T(8,128)(2,1)} reshape(bf16[16,8,2,64,128]{4,3,0,2,1:T(8,128)(2,1)} %fusion.2) | data formatting | bytes 8388608 | tf_op jit(solution)/shard_map/convert_element_type | solution.py:48
  45.9 1.9 fusion.37
  47.8 1.9 fusion.36
  49.6 1.9 fusion.35
  51.5 1.9 fusion.34
  53.4 1.9 fusion.33
  55.3 1.9 fusion.32
  57.2 1.9 fusion.31
  59.0 1.9 fusion.30
  60.9 4.9 all-to-all-start
  68.0 2.7 copy.32
  70.7 44.8 %all-to-all-done = bf16[8,16,8,2,1024]{4,1,3,2,0:T(8,128)(2,1)} async-done(((bf16[8,16,8,2,1024]{4,1,3,2,0:T(8,128)(2,1)}), bf16[8,16,8,2,1024]{4,1,3,2,0:T(8,128)(2,1)}, u32[]{:S(2)}, u32[]{:S(2)}) %all-to-all-start) | async-done | bytes 4194336 | tf_op jit(solution)/shard_map/all_to_all | solution.py:110
  115.5 8.6 %copy.26 = bf16[8,16,8,2,1024]{4,3,2,1,0:T(2,128)(2,1)} copy(bf16[8,16,8,2,1024]{4,1,3,2,0:T(8,128)(2,1)} %all-to-all-done) | data formatting | bytes 8388608 | tf_op jit(solution)/shard_map/all_to_all | solution.py:110
  124.0 7.2 %reshape_reshape.6 = bf16[16,128,1024]{2,1,0:T(8,128)(2,1)} reshape(bf16[8,16,8,2,1024]{4,3,2,1,0:T(2,128)(2,1)} %copy.26) | data formatting | bytes 8388608 | tf_op jit(solution)/shard_map/reshape;reshape | solution.py:54
  131.3 3.7 convolution_convert_fusion.3
  135.0 2.4 convolution_convert_fusion.2
  137.4 12.6 %convolution_convert_fusion.1 = bf16[4096,1024]{1,0:T(8,128)(2,1)} fusion(bf16[4096,1024]{1,0:T(8,128)(2,1)S(1)} %bitcast.162, bf16[128,8,8,128]{3,2,1,0:T(8,128)(2,1)} %bitcast.164), kind=kOutput, calls=%fused_computation.11 | convolution fusion | flops 8594128896 | bytes 18874368 | tf_op jit(solution)/shard_map/dot_general | solution.py:93
  150.1 8.0 %reshape_reshape.7 = bf16[16,262144]{1,0:T(8,128)(2,1)} reshape(bf16[4096,1024]{1,0:T(8,128)(2,1)} %convolution_convert_fusion.1) | data formatting | bytes 16777216 | tf_op jit(solution)/shard_map/reshape;reshape | solution.py:98
  158.0 13.6 %convolution_convert_fusion = bf16[32,262144]{1,0:T(8,128)(2,1)} fusion(pred[32,16]{1,0:T(32,128)(4,1)S(1)} %and.49, bf16[16,262144]{1,0:T(8,128)(2,1)} %reshape_reshape.7), kind=kOutput, calls=%fused_computation | convolution fusion | flops 276824064 | bytes 25166336 | tf_op jit(solution)/shard_map/dot_general | solution.py:98
  171.6 18.7 %copy.59 = bf16[4,8,256,1024]{3,2,1,0:T(8,128)(2,1)} copy(bf16[4,8,256,1024]{3,1,2,0:T(8,128)(2,1)} %bitcast.160) | data formatting | bytes 33554432
  190.3 7.9 %all-to-all-start.1 = ((bf16[32,2,128,1024]{3,2,1,0:T(8,128)(2,1)}), bf16[32,2,128,1024]{3,2,1,0:T(8,128)(2,1)}, u32[]{:S(2)}, u32[]{:S(2)}) async-start(bf16[32,2,128,1024]{3,2,1,0:T(8,128)(2,1)} %bitcast.159), calls=%async_computation.1 | async-start | bytes 33554432 | tf_op jit(solution)/shard_map/all_to_all | solution.py:143
  198.7 295.9 %all-to-all-done.1 = bf16[32,2,128,1024]{3,2,1,0:T(8,128)(2,1)} async-done(((bf16[32,2,128,1024]{3,2,1,0:T(8,128)(2,1)}), bf16[32,2,128,1024]{3,2,1,0:T(8,128)(2,1)}, u32[]{:S(2)}, u32[]{:S(2)}) %all-to-all-start.1) | async-done | bytes 16777248 | tf_op jit(solution)/shard_map/all_to_all | solution.py:143
  494.6 16.6 %fusion.20 = bf16[8,2,128,1024]{3,0,2,1:T(8,128)(2,1)S(1)} fusion(bf16[8,32,1,1]{0,1,3,2:T(8,128)(2,1)S(1)} %bitcast.169, bf16[2,128,1024,32]{2,1,0,3:T(8,128)(2,1)} %bitcast.83), kind=kOutput, calls=%fused_computation.22 | convolution fusion | flops 136314880 | bytes 20972032 | tf_op jit(solution)/shard_map/dot_general | solution.py:144
  511.2 4.4 copy.35
  (46 shorter events, 5.0 us)
Async XLA Ops:
  0.0 66.7 %copy-start = (bf16[8,384,128]{2,1,0:T(8,128)(2,1)S(1)}, bf16[8,384,128]{2,1,0:T(8,128)(2,1)}, u32[]{:S(2)}) copy-start(bf16[8,384,128]{2,1,0:T(8,128)(2,1)} %param.12) | copy-start | bytes 2359300
  31.0 4.7 copy-start.2
  60.9 4.9 copy-start.5
  60.9 5.3 %copy-start.3 = (bf16[2,64,64]{2,1,0:T(8,128)(2,1)S(1)}, bf16[2,64,64]{2,1,0:T(8,128)(2,1)}, u32[]{:S(2)}) copy-start(bf16[2,64,64]{2,1,0:T(8,128)(2,1)} %param.10) | copy-start | bytes 49156
  60.9 5.7 %copy-start.7 = (s32[8]{0:T(128)S(1)}, s32[8]{0:T(128)}, u32[]{:S(2)}) copy-start(s32[8]{0:T(128)} %param.13) | copy-start | bytes 100
  60.9 54.5 %all-to-all-start = ((bf16[8,16,8,2,1024]{4,1,3,2,0:T(8,128)(2,1)}), bf16[8,16,8,2,1024]{4,1,3,2,0:T(8,128)(2,1)}, u32[]{:S(2)}, u32[]{:S(2)}) async-start(bf16[8,16,8,2,1024]{4,1,3,2,0:T(8,128)(2,1)} %fusion.30), calls=%async_computation | async-start | bytes 8388608 | tf_op jit(solution)/shard_map/all_to_all | solution.py:110
  65.8 4.9 copy-start.4
  190.3 8.1 %copy-start.6 = (s32[256]{0:T(256)S(1)}, s32[256]{0:T(256)}, u32[]{:S(2)}) copy-start(s32[256]{0:T(256)} %param.15) | copy-start | bytes 3076
  190.3 304.2 %all-to-all-start.1 = ((bf16[32,2,128,1024]{3,2,1,0:T(8,128)(2,1)}), bf16[32,2,128,1024]{3,2,1,0:T(8,128)(2,1)}, u32[]{:S(2)}, u32[]{:S(2)}) async-start(bf16[32,2,128,1024]{3,2,1,0:T(8,128)(2,1)} %bitcast.159), calls=%async_computation.1 | async-start | bytes 33554432 | tf_op jit(solution)/shard_map/all_to_all | solution.py:143
  494.6 21.0 %copy-start.1 = (bf16[8,384,128]{2,1,0:T(8,128)(2,1)S(1)}, bf16[8,384,128]{2,1,0:T(8,128)(2,1)}, u32[]{:S(2)}) copy-start(bf16[8,384,128]{2,1,0:T(8,128)(2,1)} %param.12) | copy-start | bytes 2359300
